TPU v7x, 32 devices: a whole 2x2x4 slice. The times are simulated.
32 devices in a mesh: gx: 4 (over z), gy: 4 (over y, core), gz: 2 (over x).
Axes of the slice: x: 2, y: 2, z: 4, core: 2. Of those that a mesh axis runs over, the one named last changes fastest.
Arguments:
- load: bfloat16 [4, 4, 2, 64, 1152], P('gx', 'gy', 'gz'), may hold values from -6 to 6
- schur: bfloat16 [4, 4, 2, 1152, 1152], P('gx', 'gy', 'gz')
- neumann: bfloat16 [4, 4, 2, 6, 192, 192], P('gx', 'gy', 'gz')
- coarse_basis: bfloat16 [4, 4, 2, 8, 1152], P('gx', 'gy', 'gz'), may hold values from -5 to 5
- coarse_rows: bfloat16 [4, 4, 2, 8, 256], P('gx', 'gy', 'gz'), may hold values from -0.0078125 to 0.0078125
Outputs:
- iterate: bfloat16 [4, 4, 2, 64, 1152], P('gx', 'gy', 'gz')
All inputs are finite; a program needn't handle non-finite values.
Results may differ from a plain program's by a relative error of at most 0.0048.
Values sent between devices are 32-bit elements; how exact they have to be, the bound alone decides.
No kernel may reach another device: no remote copies, remote signals or barrier semaphores. Data moves between devices by JAX's collectives and lax.ppermute only.
A program may use at most 64 MiB of HBM per device.

v0:
```python
import jax
import jax.numpy as jnp
from jax import lax
from jax.sharding import PartitionSpec as P

ITERS = 2


def padded_2(shard, sides, width):
    for axis, dim in sides:
        devices, length = (lax.axis_size(axis), shard.shape[dim])
        up = [(i, (i + 1) % devices) for i in range(devices - 1)]
        down = [(j, i) for i, j in up]
        last = lax.slice_in_dim(shard, length - width, length, axis=dim)
        initial = lax.slice_in_dim(shard, 0, width, axis=dim)
        before = lax.ppermute(last, axis, up)
        after = lax.ppermute(initial, axis, down)
        shard = jnp.concatenate([before, shard, after], axis=dim)
    return shard


def x_faces(vec):
    padded = padded_2(vec[:, 0:2], (("gx", 1),), 1)
    return [padded[:, 0], padded[:, 3]]


def y_faces(vec):
    padded = padded_2(vec[:, 2:4], (("gy", 1),), 1)
    return [padded[:, 0], padded[:, 3]]


def z_faces(vec):
    padded = padded_2(vec[:, 4:6], (("gz", 1),), 1)
    return [padded[:, 0], padded[:, 3]]


def assemble(vec):
    pieces = x_faces(vec) + y_faces(vec) + z_faces(vec)
    return vec + jnp.stack(pieces, axis=1)


def side_weights(place, extent):
    lower = jnp.where(place > 0, 0.5, 1.0).astype(jnp.float32)
    upper = jnp.where(place < extent - 1, 0.5, 1.0).astype(jnp.float32)
    return [lower, upper]


def face_weights():
    values = side_weights(lax.axis_index("gx"), lax.axis_size("gx"))
    values = values + side_weights(lax.axis_index("gy"), lax.axis_size("gy"))
    values = values + side_weights(lax.axis_index("gz"), lax.axis_size("gz"))
    return jnp.stack(values).reshape(1, 6, 1)


def contract_rows(whole, rows_f):
    return lax.dot_general(whole, rows_f, (((1,), (1,)), ((), ())), precision=lax.Precision.HIGHEST)


def coarse_solve(coarse_in, rows_f):
    column = lax.all_gather(coarse_in, "gz", axis=1, tiled=True)
    whole = lax.all_gather(column, ("gx", "gy"), axis=1, tiled=True)
    return contract_rows(whole, rows_f)


def body(load, schur, neumann, coarse_basis, coarse_rows):
    count = load.shape[3]
    width = load.shape[4]
    face = width // 6
    load_f = load.reshape(count, width).astype(jnp.float32)
    schur_m = schur.reshape(width, width)
    blocks = neumann.reshape(6, face, face)
    basis = coarse_basis.reshape(coarse_basis.shape[3], width)
    basis_f = basis.astype(jnp.float32)
    rows_f = coarse_rows.reshape(coarse_rows.shape[3], coarse_rows.shape[4]).astype(jnp.float32)
    weight = face_weights()
    iterate = jnp.zeros((count, width), jnp.float32)
    for step in range(ITERS):
        if step == 0:
            local = load_f
        else:
            local = load_f - jnp.dot(
                iterate.astype(jnp.bfloat16), schur_m, preferred_element_type=jnp.float32
            )
        resid = assemble(local.reshape(count, 6, face))
        scaled = (resid * weight).astype(jnp.bfloat16)
        flat = scaled.reshape(count, width)
        coarse_in = lax.dot_general(
            flat, basis, (((1,), (1,)), ((), ())), preferred_element_type=jnp.float32
        )
        coarse_out = coarse_solve(coarse_in, rows_f)
        local_part = jnp.einsum("rfa,fab->rfb", scaled, blocks, preferred_element_type=jnp.float32)
        coarse_part = jnp.dot(coarse_out, basis_f, precision=lax.Precision.HIGHEST)
        correction = local_part + coarse_part.reshape(count, 6, face)
        update = assemble(correction * weight)
        iterate = iterate + 0.5 * update.reshape(count, width)
    return iterate.astype(jnp.bfloat16).reshape(load.shape)


def solution(mesh):
    placed = (
        P("gx", "gy", "gz", None, None),
        P("gx", "gy", "gz", None, None),
        P("gx", "gy", "gz", None, None, None),
        P("gx", "gy", "gz", None, None),
        P("gx", "gy", "gz", None, None),
    )
    return jax.shard_map(
        body, mesh=mesh, in_specs=placed, out_specs=P("gx", "gy", "gz", None, None), check_vma=False
    )
```

profile of v0, /device:TPU:0, one launch (start us, length us, event | category | flops | bytes accessed | tf_op | source)
XLA Modules:
  0.0 143.1 jit_solution(15394782454922018203)
XLA Ops:
  2.1 5.6 %collective-permute-start = (f32[64,1,192]{2,0,1:T(8,128)}, f32[64,1,192]{2,0,1:T(8,128)}, u32[]{:S(2)}, u32[]{:S(2)}) collective-permute-start(f32[64,1,192]{2,0,1:T(8,128)} %get-tuple-element.30), channel_id=1, source_target_pairs={{0,8},{8,16},{16,24},{1,9},{9,17},{17,25},{2,10},{10,18},{18,26},{... | collective-permute-start | bytes 147464 | tf_op jit(solution)/shard_map/ppermute | solution.py:16
  7.7 1.3 collective-permute-start.1
  9.0 2.1 %collective-permute-start.2 = (f32[64,1,192]{2,0,1:T(8,128)S(1)}, f32[64,1,192]{2,0,1:T(8,128)}, u32[]{:S(2)}, u32[]{:S(2)}) collective-permute-start(f32[64,1,192]{2,0,1:T(8,128)S(1)} %get-tuple-element.28), channel_id=1, source_target_pairs={{0,2},{2,4},{4,6},{1,3},{3,5},{5,7},{8,10},{10,12},{12,14},{9,11},... | collective-permute-start | bytes 147464 | tf_op jit(solution)/shard_map/ppermute | solution.py:16
  11.0 1.3 collective-permute-start.3
  12.3 4.0 %collective-permute-start.4 = (f32[64,1,192]{2,0,1:T(8,128)S(1)}, f32[64,1,192]{2,0,1:T(8,128)}, u32[]{:S(2)}, u32[]{:S(2)}) collective-permute-start(f32[64,1,192]{2,0,1:T(8,128)S(1)} %get-tuple-element.26), channel_id=1, source_target_pairs={{0,1},{2,3},{4,5},{6,7},{8,9},{10,11},{12,13},{14,15},{16,17},{18,... | collective-permute-start | bytes 147464 | tf_op jit(solution)/shard_map/ppermute | solution.py:16
  17.3 1.4 collective-permute-start.5
  24.4 4.4 %all_gather.12 = f32[64,16]{0,1:T(8,128)S(1)} all-gather(f32[64,8]{0,1:T(8,128)S(1)} %fusion.13), channel_id=1, replica_groups=mesh['gx'=4,'gy'=4,'gz'=2] {'gz'}, dimensions={1}, use_global_device_ids=true | all-gather | bytes 6144 | tf_op jit(solution)/shard_map/all_gather | solution.py:60
  28.8 25.3 %all_gather.13 = f32[64,256]{0,1:T(8,128)S(1)} all-gather(f32[64,16]{0,1:T(8,128)S(1)} %all_gather.12), channel_id=1, replica_groups=mesh['gx'=4,'gy'=4,'gz'=2] {'gx','gy'}, dimensions={1}, use_global_device_ids=true | all-gather | bytes 69632 | tf_op jit(solution)/shard_map/all_gather | solution.py:61
  54.6 1.3 collective-permute-start.6
  55.9 1.3 collective-permute-start.7
  57.2 2.3 %collective-permute-start.8 = (f32[64,1,192]{2,0,1:T(8,128)S(1)}, f32[64,1,192]{2,0,1:T(8,128)S(1)}, u32[]{:S(2)}, u32[]{:S(2)}) collective-permute-start(f32[64,1,192]{2,0,1:T(8,128)S(1)} %get-tuple-element.22), channel_id=1, source_target_pairs={{0,2},{2,4},{4,6},{1,3},{3,5},{5,7},{8,10},{10,12},{12,14},{9,11},... | collective-permute-start | bytes 147464 | tf_op jit(solution)/shard_map/ppermute | solution.py:16
  59.5 1.3 collective-permute-start.9
  60.8 3.9 %collective-permute-start.10 = (f32[64,1,192]{2,0,1:T(8,128)S(1)}, f32[64,1,192]{2,0,1:T(8,128)S(1)}, u32[]{:S(2)}, u32[]{:S(2)}) collective-permute-start(f32[64,1,192]{2,0,1:T(8,128)S(1)} %get-tuple-element.20), channel_id=1, source_target_pairs={{0,1},{2,3},{4,5},{6,7},{8,9},{10,11},{12,13},{14,15},{16,17},{18,... | collective-permute-start | bytes 147464 | tf_op jit(solution)/shard_map/ppermute | solution.py:16
  64.8 1.3 collective-permute-start.11
  67.1 4.4 %collective-permute-done.11 = f32[64,1,192]{2,0,1:T(8,128)S(1)} collective-permute-done((f32[64,1,192]{2,0,1:T(8,128)S(1)}, f32[64,1,192]{2,0,1:T(8,128)S(1)}, u32[]{:S(2)}, u32[]{:S(2)}) %collective-permute-start.11) | collective-permute-done | bytes 49184 | tf_op jit(solution)/shard_map/ppermute | solution.py:17
  76.1 4.9 %collective-permute-start.12 = (f32[64,1,192]{2,0,1:T(8,128)}, f32[64,1,192]{2,0,1:T(8,128)}, u32[]{:S(2)}, u32[]{:S(2)}) collective-permute-start(f32[64,1,192]{2,0,1:T(8,128)} %get-tuple-element.18), channel_id=1, source_target_pairs={{0,8},{8,16},{16,24},{1,9},{9,17},{17,25},{2,10},{10,18},{18,26},{... | collective-permute-start | bytes 147464 | tf_op jit(solution)/shard_map/ppermute | solution.py:16
  82.4 1.6 %collective-permute-start.14 = (f32[64,1,192]{2,0,1:T(8,128)}, f32[64,1,192]{2,0,1:T(8,128)S(1)}, u32[]{:S(2)}, u32[]{:S(2)}) collective-permute-start(f32[64,1,192]{2,0,1:T(8,128)} %get-tuple-element.16), channel_id=1, source_target_pairs={{0,2},{2,4},{4,6},{1,3},{3,5},{5,7},{8,10},{10,12},{12,14},{9,11},... | collective-permute-start | bytes 147464 | tf_op jit(solution)/shard_map/ppermute | solution.py:16
  84.0 1.3 collective-permute-start.15
  85.3 1.5 %collective-permute-start.16 = (f32[64,1,192]{2,0,1:T(8,128)S(1)}, f32[64,1,192]{2,0,1:T(8,128)S(1)}, u32[]{:S(2)}, u32[]{:S(2)}) collective-permute-start(f32[64,1,192]{2,0,1:T(8,128)S(1)} %get-tuple-element.14), channel_id=1, source_target_pairs={{0,1},{2,3},{4,5},{6,7},{8,9},{10,11},{12,13},{14,15},{16,17},{18,... | collective-permute-start | bytes 147464 | tf_op jit(solution)/shard_map/ppermute | solution.py:16
  86.8 1.3 collective-permute-start.17
  89.0 3.9 %collective-permute-done.17 = f32[64,1,192]{2,0,1:T(8,128)S(1)} collective-permute-done((f32[64,1,192]{2,0,1:T(8,128)S(1)}, f32[64,1,192]{2,0,1:T(8,128)S(1)}, u32[]{:S(2)}, u32[]{:S(2)}) %collective-permute-start.17) | collective-permute-done | bytes 49184 | tf_op jit(solution)/shard_map/ppermute | solution.py:17
  93.0 2.1 %convolution_bitcast_fusion = f32[64,6,192]{2,0,1:T(8,128)} fusion(bf16[1,1,1,6,192,192]{5,4,3,2,1,0:T(8,128)(2,1)} %param.7, f32[64,6,192]{2,0,1:T(8,128)S(1)} %copy.44, f32[64,6,192]{2,0,1:T(8,128)S(1)} %constant_dynamic-update-slice_fusion.12, f32[6]{0:T(128)S(1)} %stack.42), kind=kOutput, calls=%fused_computation.5 | convolution fusion | flops 28532736 | bytes 1327128 | tf_op jit(solution)/shard_map/rfa,fab->rfb/dot_general | solution.py:91
  97.3 4.4 %all_gather.14 = f32[64,16]{0,1:T(8,128)S(1)} all-gather(f32[64,8]{0,1:T(8,128)S(1)} %fusion.10), channel_id=1, replica_groups=mesh['gx'=4,'gy'=4,'gz'=2] {'gz'}, dimensions={1}, use_global_device_ids=true | all-gather | bytes 6144 | tf_op jit(solution)/shard_map/all_gather | solution.py:60
  101.7 23.9 %all_gather.15 = f32[64,256]{0,1:T(8,128)S(1)} all-gather(f32[64,16]{0,1:T(8,128)S(1)} %all_gather.14), channel_id=1, replica_groups=mesh['gx'=4,'gy'=4,'gz'=2] {'gx','gy'}, dimensions={1}, use_global_device_ids=true | all-gather | bytes 69632 | tf_op jit(solution)/shard_map/all_gather | solution.py:61
  125.8 1.4 fusion.5
  127.2 1.3 collective-permute-start.18
  128.5 1.3 collective-permute-start.19
  129.8 2.2 %collective-permute-start.20 = (f32[64,1,192]{2,0,1:T(8,128)S(1)}, f32[64,1,192]{2,0,1:T(8,128)S(1)}, u32[]{:S(2)}, u32[]{:S(2)}) collective-permute-start(f32[64,1,192]{2,0,1:T(8,128)S(1)} %get-tuple-element.10), channel_id=1, source_target_pairs={{0,2},{2,4},{4,6},{1,3},{3,5},{5,7},{8,10},{10,12},{12,14},{9,11},... | collective-permute-start | bytes 147464 | tf_op jit(solution)/shard_map/ppermute | solution.py:16
  132.1 1.3 collective-permute-start.21
  133.4 1.9 %collective-permute-start.22 = (f32[64,1,192]{2,0,1:T(8,128)S(1)}, f32[64,1,192]{2,0,1:T(8,128)S(1)}, u32[]{:S(2)}, u32[]{:S(2)}) collective-permute-start(f32[64,1,192]{2,0,1:T(8,128)S(1)} %get-tuple-element.8), channel_id=1, source_target_pairs={{0,1},{2,3},{4,5},{6,7},{8,9},{10,11},{12,13},{14,15},{16,17},{18,... | collective-permute-start | bytes 147464 | tf_op jit(solution)/shard_map/ppermute | solution.py:16
  135.3 1.3 collective-permute-start.23
  137.6 4.4 %collective-permute-done.23 = f32[64,1,192]{2,0,1:T(8,128)S(1)} collective-permute-done((f32[64,1,192]{2,0,1:T(8,128)S(1)}, f32[64,1,192]{2,0,1:T(8,128)S(1)}, u32[]{:S(2)}, u32[]{:S(2)}) %collective-permute-start.23) | collective-permute-done | bytes 49184 | tf_op jit(solution)/shard_map/ppermute | solution.py:17
  (88 shorter events, 21.5 us)
Async XLA Ops:
  0.0 72.6 %copy-start = (bf16[1,1,1,1152,1152]{4,3,2,1,0:T(8,128)(2,1)S(1)}, bf16[1,1,1,1152,1152]{4,3,2,1,0:T(8,128)(2,1)}, u32[]{:S(2)}) copy-start(bf16[1,1,1,1152,1152]{4,3,2,1,0:T(8,128)(2,1)} %param.6) | copy-start | bytes 7962628
  1.4 22.9 %copy-start.4 = (bf16[1,1,1,8,1152]{4,3,2,1,0:T(8,128)(2,1)S(1)}, bf16[1,1,1,8,1152]{4,3,2,1,0:T(8,128)(2,1)}, u32[]{:S(2)}) copy-start(bf16[1,1,1,8,1152]{4,3,2,1,0:T(8,128)(2,1)} %param.8) | copy-start | bytes 55300
  1.4 52.6 %copy-start.5 = (bf16[1,1,1,8,256]{4,3,2,1,0:T(8,128)(2,1)S(1)}, bf16[1,1,1,8,256]{4,3,2,1,0:T(8,128)(2,1)}, u32[]{:S(2)}) copy-start(bf16[1,1,1,8,256]{4,3,2,1,0:T(8,128)(2,1)} %param.9) | copy-start | bytes 12292
  2.1 15.2 %collective-permute-start = (f32[64,1,192]{2,0,1:T(8,128)}, f32[64,1,192]{2,0,1:T(8,128)}, u32[]{:S(2)}, u32[]{:S(2)}) collective-permute-start(f32[64,1,192]{2,0,1:T(8,128)} %get-tuple-element.30), channel_id=1, source_target_pairs={{0,8},{8,16},{16,24},{1,9},{9,17},{17,25},{2,10},{10,18},{18,26},{... | collective-permute-start | bytes 147464 | tf_op jit(solution)/shard_map/ppermute | solution.py:16
  7.7 11.9 %collective-permute-start.1 = (f32[64,1,192]{2,0,1:T(8,128)}, f32[64,1,192]{2,0,1:T(8,128)}, u32[]{:S(2)}, u32[]{:S(2)}) collective-permute-start(f32[64,1,192]{2,0,1:T(8,128)} %get-tuple-element.29), channel_id=1, source_target_pairs={{8,0},{16,8},{24,16},{9,1},{17,9},{25,17},{10,2},{18,10},{26,18},{... | collective-permute-start | bytes 147464 | tf_op jit(solution)/shard_map/ppermute | solution.py:17
  9.0 11.4 %collective-permute-start.2 = (f32[64,1,192]{2,0,1:T(8,128)S(1)}, f32[64,1,192]{2,0,1:T(8,128)}, u32[]{:S(2)}, u32[]{:S(2)}) collective-permute-start(f32[64,1,192]{2,0,1:T(8,128)S(1)} %get-tuple-element.28), channel_id=1, source_target_pairs={{0,2},{2,4},{4,6},{1,3},{3,5},{5,7},{8,10},{10,12},{12,14},{9,11},... | collective-permute-start | bytes 147464 | tf_op jit(solution)/shard_map/ppermute | solution.py:16
  11.0 10.2 %collective-permute-start.3 = (f32[64,1,192]{2,0,1:T(8,128)S(1)}, f32[64,1,192]{2,0,1:T(8,128)}, u32[]{:S(2)}, u32[]{:S(2)}) collective-permute-start(f32[64,1,192]{2,0,1:T(8,128)S(1)} %get-tuple-element.27), channel_id=1, source_target_pairs={{2,0},{4,2},{6,4},{3,1},{5,3},{7,5},{10,8},{12,10},{14,12},{11,9},... | collective-permute-start | bytes 147464 | tf_op jit(solution)/shard_map/ppermute | solution.py:17
  12.3 9.8 %collective-permute-start.4 = (f32[64,1,192]{2,0,1:T(8,128)S(1)}, f32[64,1,192]{2,0,1:T(8,128)}, u32[]{:S(2)}, u32[]{:S(2)}) collective-permute-start(f32[64,1,192]{2,0,1:T(8,128)S(1)} %get-tuple-element.26), channel_id=1, source_target_pairs={{0,1},{2,3},{4,5},{6,7},{8,9},{10,11},{12,13},{14,15},{16,17},{18,... | collective-permute-start | bytes 147464 | tf_op jit(solution)/shard_map/ppermute | solution.py:16
  17.3 6.6 %copy-start.1 = (bf16[1,1,1,6,192,192]{5,4,3,2,1,0:T(8,128)(2,1)S(1)}, bf16[1,1,1,6,192,192]{5,4,3,2,1,0:T(8,128)(2,1)}, u32[]{:S(2)}) copy-start(bf16[1,1,1,6,192,192]{5,4,3,2,1,0:T(8,128)(2,1)} %param.7) | copy-start | bytes 1327108
  17.3 6.3 %collective-permute-start.5 = (f32[64,1,192]{2,0,1:T(8,128)S(1)}, f32[64,1,192]{2,0,1:T(8,128)S(1)}, u32[]{:S(2)}, u32[]{:S(2)}) collective-permute-start(f32[64,1,192]{2,0,1:T(8,128)S(1)} %get-tuple-element.25), channel_id=1, source_target_pairs={{1,0},{3,2},{5,4},{7,6},{9,8},{11,10},{13,12},{15,14},{17,16},{19,... | collective-permute-start | bytes 147464 | tf_op jit(solution)/shard_map/ppermute | solution.py:17
  24.3 48.3 %copy-start.3 = (bf16[1,1,1,64,1152]{4,3,2,1,0:T(8,128)(2,1)S(1)}, bf16[1,1,1,64,1152]{4,3,2,1,0:T(8,128)(2,1)}, u32[]{:S(2)}) copy-start(bf16[1,1,1,64,1152]{4,3,2,1,0:T(8,128)(2,1)} %param.5) | copy-start | bytes 442372
  54.6 10.1 %collective-permute-start.6 = (f32[64,1,192]{2,0,1:T(8,128)S(1)}, f32[64,1,192]{2,0,1:T(8,128)S(1)}, u32[]{:S(2)}, u32[]{:S(2)}) collective-permute-start(f32[64,1,192]{2,0,1:T(8,128)S(1)} %get-tuple-element.24), channel_id=1, source_target_pairs={{0,8},{8,16},{16,24},{1,9},{9,17},{17,25},{2,10},{10,18},{18,26},{... | collective-permute-start | bytes 147464 | tf_op jit(solution)/shard_map/ppermute | solution.py:16
  55.9 10.1 %collective-permute-start.7 = (f32[64,1,192]{2,0,1:T(8,128)S(1)}, f32[64,1,192]{2,0,1:T(8,128)S(1)}, u32[]{:S(2)}, u32[]{:S(2)}) collective-permute-start(f32[64,1,192]{2,0,1:T(8,128)S(1)} %get-tuple-element.23), channel_id=1, source_target_pairs={{8,0},{16,8},{24,16},{9,1},{17,9},{25,17},{10,2},{18,10},{26,18},{... | collective-permute-start | bytes 147464 | tf_op jit(solution)/shard_map/ppermute | solution.py:17
  57.2 8.9 %collective-permute-start.8 = (f32[64,1,192]{2,0,1:T(8,128)S(1)}, f32[64,1,192]{2,0,1:T(8,128)S(1)}, u32[]{:S(2)}, u32[]{:S(2)}) collective-permute-start(f32[64,1,192]{2,0,1:T(8,128)S(1)} %get-tuple-element.22), channel_id=1, source_target_pairs={{0,2},{2,4},{4,6},{1,3},{3,5},{5,7},{8,10},{10,12},{12,14},{9,11},... | collective-permute-start | bytes 147464 | tf_op jit(solution)/shard_map/ppermute | solution.py:16
  59.5 6.6 %collective-permute-start.9 = (f32[64,1,192]{2,0,1:T(8,128)S(1)}, f32[64,1,192]{2,0,1:T(8,128)S(1)}, u32[]{:S(2)}, u32[]{:S(2)}) collective-permute-start(f32[64,1,192]{2,0,1:T(8,128)S(1)} %get-tuple-element.21), channel_id=1, source_target_pairs={{2,0},{4,2},{6,4},{3,1},{5,3},{7,5},{10,8},{12,10},{14,12},{11,9},... | collective-permute-start | bytes 147464 | tf_op jit(solution)/shard_map/ppermute | solution.py:17
  60.8 6.3 %collective-permute-start.10 = (f32[64,1,192]{2,0,1:T(8,128)S(1)}, f32[64,1,192]{2,0,1:T(8,128)S(1)}, u32[]{:S(2)}, u32[]{:S(2)}) collective-permute-start(f32[64,1,192]{2,0,1:T(8,128)S(1)} %get-tuple-element.20), channel_id=1, source_target_pairs={{0,1},{2,3},{4,5},{6,7},{8,9},{10,11},{12,13},{14,15},{16,17},{18,... | collective-permute-start | bytes 147464 | tf_op jit(solution)/shard_map/ppermute | solution.py:16
  64.8 6.7 %collective-permute-start.11 = (f32[64,1,192]{2,0,1:T(8,128)S(1)}, f32[64,1,192]{2,0,1:T(8,128)S(1)}, u32[]{:S(2)}, u32[]{:S(2)}) collective-permute-start(f32[64,1,192]{2,0,1:T(8,128)S(1)} %get-tuple-element.19), channel_id=1, source_target_pairs={{1,0},{3,2},{5,4},{7,6},{9,8},{11,10},{13,12},{15,14},{17,16},{19,... | collective-permute-start | bytes 147464 | tf_op jit(solution)/shard_map/ppermute | solution.py:17
  76.1 10.7 %collective-permute-start.12 = (f32[64,1,192]{2,0,1:T(8,128)}, f32[64,1,192]{2,0,1:T(8,128)}, u32[]{:S(2)}, u32[]{:S(2)}) collective-permute-start(f32[64,1,192]{2,0,1:T(8,128)} %get-tuple-element.18), channel_id=1, source_target_pairs={{0,8},{8,16},{16,24},{1,9},{9,17},{17,25},{2,10},{10,18},{18,26},{... | collective-permute-start | bytes 147464 | tf_op jit(solution)/shard_map/ppermute | solution.py:16
  81.1 7.8 %collective-permute-start.13 = (f32[64,1,192]{2,0,1:T(8,128)}, f32[64,1,192]{2,0,1:T(8,128)S(1)}, u32[]{:S(2)}, u32[]{:S(2)}) collective-permute-start(f32[64,1,192]{2,0,1:T(8,128)} %get-tuple-element.17), channel_id=1, source_target_pairs={{8,0},{16,8},{24,16},{9,1},{17,9},{25,17},{10,2},{18,10},{26,18},{... | collective-permute-start | bytes 147464 | tf_op jit(solution)/shard_map/ppermute | solution.py:17
  82.4 6.6 %collective-permute-start.14 = (f32[64,1,192]{2,0,1:T(8,128)}, f32[64,1,192]{2,0,1:T(8,128)S(1)}, u32[]{:S(2)}, u32[]{:S(2)}) collective-permute-start(f32[64,1,192]{2,0,1:T(8,128)} %get-tuple-element.16), channel_id=1, source_target_pairs={{0,2},{2,4},{4,6},{1,3},{3,5},{5,7},{8,10},{10,12},{12,14},{9,11},... | collective-permute-start | bytes 147464 | tf_op jit(solution)/shard_map/ppermute | solution.py:16
  84.0 5.0 %collective-permute-start.15 = (f32[64,1,192]{2,0,1:T(8,128)}, f32[64,1,192]{2,0,1:T(8,128)S(1)}, u32[]{:S(2)}, u32[]{:S(2)}) collective-permute-start(f32[64,1,192]{2,0,1:T(8,128)} %get-tuple-element.15), channel_id=1, source_target_pairs={{2,0},{4,2},{6,4},{3,1},{5,3},{7,5},{10,8},{12,10},{14,12},{11,9},... | collective-permute-start | bytes 147464 | tf_op jit(solution)/shard_map/ppermute | solution.py:17
  85.3 3.7 %collective-permute-start.16 = (f32[64,1,192]{2,0,1:T(8,128)S(1)}, f32[64,1,192]{2,0,1:T(8,128)S(1)}, u32[]{:S(2)}, u32[]{:S(2)}) collective-permute-start(f32[64,1,192]{2,0,1:T(8,128)S(1)} %get-tuple-element.14), channel_id=1, source_target_pairs={{0,1},{2,3},{4,5},{6,7},{8,9},{10,11},{12,13},{14,15},{16,17},{18,... | collective-permute-start | bytes 147464 | tf_op jit(solution)/shard_map/ppermute | solution.py:16
  86.8 6.2 %collective-permute-start.17 = (f32[64,1,192]{2,0,1:T(8,128)S(1)}, f32[64,1,192]{2,0,1:T(8,128)S(1)}, u32[]{:S(2)}, u32[]{:S(2)}) collective-permute-start(f32[64,1,192]{2,0,1:T(8,128)S(1)} %get-tuple-element.13), channel_id=1, source_target_pairs={{1,0},{3,2},{5,4},{7,6},{9,8},{11,10},{13,12},{15,14},{17,16},{19,... | collective-permute-start | bytes 147464 | tf_op jit(solution)/shard_map/ppermute | solution.py:17
  96.2 45.9 %copy-start.2 = (f32[64,6,192]{2,0,1:T(8,128)S(1)}, f32[64,6,192]{2,0,1:T(8,128)}, u32[]{:S(2)}) copy-start(f32[64,6,192]{2,0,1:T(8,128)} %get-tuple-element.6) | copy-start | bytes 884740
  127.2 8.1 %collective-permute-start.18 = (f32[64,1,192]{2,0,1:T(8,128)S(1)}, f32[64,1,192]{2,0,1:T(8,128)S(1)}, u32[]{:S(2)}, u32[]{:S(2)}) collective-permute-start(f32[64,1,192]{2,0,1:T(8,128)S(1)} %get-tuple-element.12), channel_id=1, source_target_pairs={{0,8},{8,16},{16,24},{1,9},{9,17},{17,25},{2,10},{10,18},{18,26},{... | collective-permute-start | bytes 147464 | tf_op jit(solution)/shard_map/ppermute | solution.py:16
  128.5 8.1 %collective-permute-start.19 = (f32[64,1,192]{2,0,1:T(8,128)S(1)}, f32[64,1,192]{2,0,1:T(8,128)S(1)}, u32[]{:S(2)}, u32[]{:S(2)}) collective-permute-start(f32[64,1,192]{2,0,1:T(8,128)S(1)} %get-tuple-element.11), channel_id=1, source_target_pairs={{8,0},{16,8},{24,16},{9,1},{17,9},{25,17},{10,2},{18,10},{26,18},{... | collective-permute-start | bytes 147464 | tf_op jit(solution)/shard_map/ppermute | solution.py:17
  129.8 6.8 %collective-permute-start.20 = (f32[64,1,192]{2,0,1:T(8,128)S(1)}, f32[64,1,192]{2,0,1:T(8,128)S(1)}, u32[]{:S(2)}, u32[]{:S(2)}) collective-permute-start(f32[64,1,192]{2,0,1:T(8,128)S(1)} %get-tuple-element.10), channel_id=1, source_target_pairs={{0,2},{2,4},{4,6},{1,3},{3,5},{5,7},{8,10},{10,12},{12,14},{9,11},... | collective-permute-start | bytes 147464 | tf_op jit(solution)/shard_map/ppermute | solution.py:16
  132.1 4.6 %collective-permute-start.21 = (f32[64,1,192]{2,0,1:T(8,128)S(1)}, f32[64,1,192]{2,0,1:T(8,128)S(1)}, u32[]{:S(2)}, u32[]{:S(2)}) collective-permute-start(f32[64,1,192]{2,0,1:T(8,128)S(1)} %get-tuple-element.9), channel_id=1, source_target_pairs={{2,0},{4,2},{6,4},{3,1},{5,3},{7,5},{10,8},{12,10},{14,12},{11,9},... | collective-permute-start | bytes 147464 | tf_op jit(solution)/shard_map/ppermute | solution.py:17
  133.4 4.2 %collective-permute-start.22 = (f32[64,1,192]{2,0,1:T(8,128)S(1)}, f32[64,1,192]{2,0,1:T(8,128)S(1)}, u32[]{:S(2)}, u32[]{:S(2)}) collective-permute-start(f32[64,1,192]{2,0,1:T(8,128)S(1)} %get-tuple-element.8), channel_id=1, source_target_pairs={{0,1},{2,3},{4,5},{6,7},{8,9},{10,11},{12,13},{14,15},{16,17},{18,... | collective-permute-start | bytes 147464 | tf_op jit(solution)/shard_map/ppermute | solution.py:16
  135.3 6.7 %collective-permute-start.23 = (f32[64,1,192]{2,0,1:T(8,128)S(1)}, f32[64,1,192]{2,0,1:T(8,128)S(1)}, u32[]{:S(2)}, u32[]{:S(2)}) collective-permute-start(f32[64,1,192]{2,0,1:T(8,128)S(1)} %get-tuple-element.7), channel_id=1, source_target_pairs={{1,0},{3,2},{5,4},{7,6},{9,8},{11,10},{13,12},{15,14},{17,16},{19,... | collective-permute-start | bytes 147464 | tf_op jit(solution)/shard_map/ppermute | solution.py:17
where the time goes:
time: 144 us; the launch traced here: 143 us
  blocking collectives  58 us (40%)
  starting transfers between devices  48.1 us (33%)
  waiting for transfers between devices  15.3 us (11%)
  local copies, waits for them, and re-layouts  13.9 us (10%)
  matrix products  6.25 us (4%)
    all_gather x2, blocking collectives, coarse_solve(): whole = lax.all_gather(column, ('gx', 'gy'), axis=1, tiled=True)  49.2 us
    ppermute x12, starting transfers between devices, padded_2(): before = lax.ppermute(last, axis, up)  32.5 us
    ppermute x12, starting transfers between devices, padded_2(): after = lax.ppermute(initial, axis, down)  15.6 us
    ppermute x12, waiting for transfers between devices, padded_2(): after = lax.ppermute(initial, axis, down)  13.4 us
    all_gather x2, blocking collectives, coarse_solve(): column = lax.all_gather(coarse_in, 'gz', axis=1, tiled=True)  8.77 us
    unnamed x32, local copies, waits for them, and re-layouts  5.19 us
  transfers between devices with their start and end apart: 24, of which 6 were waited for; matrix products, arithmetic and copies ran while one was open for 4% of the time, Pallas kernels for 0%

commit v1 on v0

--- a/solution.py
+++ b/solution.py
@@ -57,7 +57,7 @@
 
 
 def coarse_solve(coarse_in, rows_f):
-    column = lax.all_gather(coarse_in, "gz", axis=1, tiled=True)
+    column = jnp.concatenate(lax.all_gather(coarse_in, axis_name="gz"), axis=1)
     whole = lax.all_gather(column, ("gx", "gy"), axis=1, tiled=True)
     return contract_rows(whole, rows_f)
 

time: 144 us -> 144 us (level)
  no operation moved by 1% of the time
where the time goes in v1:
time: 144 us; the launch traced here: 143 us
  blocking collectives  58 us (40%)
  starting transfers between devices  48.1 us (33%)
  waiting for transfers between devices  15.3 us (11%)
  local copies, waits for them, and re-layouts  13.9 us (10%)
  matrix products  6.25 us (4%)
    all_gather x2, blocking collectives, coarse_solve(): whole = lax.all_gather(column, ('gx', 'gy'), axis=1, tiled=True)  49.2 us
    ppermute x12, starting transfers between devices, padded_2(): before = lax.ppermute(last, axis, up)  32.5 us
    ppermute x12, starting transfers between devices, padded_2(): after = lax.ppermute(initial, axis, down)  15.6 us
    ppermute x12, waiting for transfers between devices, padded_2(): after = lax.ppermute(initial, axis, down)  13.4 us
    all_gather x2, blocking collectives, coarse_solve(): column = jnp.concatenate(lax.all_gather(coarse_in, axis_name='gz'), axis=1)  8.77 us
    unnamed x32, local copies, waits for them, and re-layouts  5.19 us
  transfers between devices with their start and end apart: 24, of which 6 were waited for; matrix products, arithmetic and copies ran while one was open for 4% of the time, Pallas kernels for 0%

profile of v1, /device:TPU:0, one launch (start us, length us, event | category | flops | bytes accessed | tf_op | source)
XLA Modules:
  0.0 143.1 jit_solution(7194089165420671859)
XLA Ops:
  2.1 5.6 %collective-permute-start = (f32[64,1,192]{2,0,1:T(8,128)}, f32[64,1,192]{2,0,1:T(8,128)}, u32[]{:S(2)}, u32[]{:S(2)}) collective-permute-start(f32[64,1,192]{2,0,1:T(8,128)} %get-tuple-element.30), channel_id=1, source_target_pairs={{0,8},{8,16},{16,24},{1,9},{9,17},{17,25},{2,10},{10,18},{18,26},{... | collective-permute-start | bytes 147464 | tf_op jit(solution)/shard_map/ppermute | solution.py:16
  7.7 1.3 collective-permute-start.1
  9.0 2.1 %collective-permute-start.2 = (f32[64,1,192]{2,0,1:T(8,128)S(1)}, f32[64,1,192]{2,0,1:T(8,128)}, u32[]{:S(2)}, u32[]{:S(2)}) collective-permute-start(f32[64,1,192]{2,0,1:T(8,128)S(1)} %get-tuple-element.28), channel_id=1, source_target_pairs={{0,2},{2,4},{4,6},{1,3},{3,5},{5,7},{8,10},{10,12},{12,14},{9,11},... | collective-permute-start | bytes 147464 | tf_op jit(solution)/shard_map/ppermute | solution.py:16
  11.0 1.3 collective-permute-start.3
  12.3 4.0 %collective-permute-start.4 = (f32[64,1,192]{2,0,1:T(8,128)S(1)}, f32[64,1,192]{2,0,1:T(8,128)}, u32[]{:S(2)}, u32[]{:S(2)}) collective-permute-start(f32[64,1,192]{2,0,1:T(8,128)S(1)} %get-tuple-element.26), channel_id=1, source_target_pairs={{0,1},{2,3},{4,5},{6,7},{8,9},{10,11},{12,13},{14,15},{16,17},{18,... | collective-permute-start | bytes 147464 | tf_op jit(solution)/shard_map/ppermute | solution.py:16
  17.3 1.4 collective-permute-start.5
  24.4 4.4 %all-gather.2 = f32[2,64,8]{1,2,0:T(8,128)S(1)} all-gather(f32[1,64,8]{1,2,0:T(8,128)S(1)} %convolution_bitcast_fusion.5), channel_id=2, replica_groups=mesh['gx'=4,'gy'=4,'gz'=2] {'gz'}, dimensions={0}, use_global_device_ids=true | all-gather | bytes 6144 | tf_op jit(solution)/shard_map/all_gather | solution.py:60
  28.8 25.3 %all_gather.20 = f32[64,256]{0,1:T(8,128)S(1)} all-gather(f32[64,16]{0,1:T(8,128)S(1)} %bitcast.60), channel_id=1, replica_groups=mesh['gx'=4,'gy'=4,'gz'=2] {'gx','gy'}, dimensions={1}, use_global_device_ids=true | all-gather | bytes 69632 | tf_op jit(solution)/shard_map/all_gather | solution.py:61
  54.6 1.3 collective-permute-start.6
  55.9 1.3 collective-permute-start.7
  57.2 2.3 %collective-permute-start.8 = (f32[64,1,192]{2,0,1:T(8,128)S(1)}, f32[64,1,192]{2,0,1:T(8,128)S(1)}, u32[]{:S(2)}, u32[]{:S(2)}) collective-permute-start(f32[64,1,192]{2,0,1:T(8,128)S(1)} %get-tuple-element.22), channel_id=1, source_target_pairs={{0,2},{2,4},{4,6},{1,3},{3,5},{5,7},{8,10},{10,12},{12,14},{9,11},... | collective-permute-start | bytes 147464 | tf_op jit(solution)/shard_map/ppermute | solution.py:16
  59.5 1.3 collective-permute-start.9
  60.8 3.9 %collective-permute-start.10 = (f32[64,1,192]{2,0,1:T(8,128)S(1)}, f32[64,1,192]{2,0,1:T(8,128)S(1)}, u32[]{:S(2)}, u32[]{:S(2)}) collective-permute-start(f32[64,1,192]{2,0,1:T(8,128)S(1)} %get-tuple-element.20), channel_id=1, source_target_pairs={{0,1},{2,3},{4,5},{6,7},{8,9},{10,11},{12,13},{14,15},{16,17},{18,... | collective-permute-start | bytes 147464 | tf_op jit(solution)/shard_map/ppermute | solution.py:16
  64.8 1.3 collective-permute-start.11
  67.1 4.4 %collective-permute-done.11 = f32[64,1,192]{2,0,1:T(8,128)S(1)} collective-permute-done((f32[64,1,192]{2,0,1:T(8,128)S(1)}, f32[64,1,192]{2,0,1:T(8,128)S(1)}, u32[]{:S(2)}, u32[]{:S(2)}) %collective-permute-start.11) | collective-permute-done | bytes 49184 | tf_op jit(solution)/shard_map/ppermute | solution.py:17
  76.1 4.9 %collective-permute-start.12 = (f32[64,1,192]{2,0,1:T(8,128)}, f32[64,1,192]{2,0,1:T(8,128)}, u32[]{:S(2)}, u32[]{:S(2)}) collective-permute-start(f32[64,1,192]{2,0,1:T(8,128)} %get-tuple-element.18), channel_id=1, source_target_pairs={{0,8},{8,16},{16,24},{1,9},{9,17},{17,25},{2,10},{10,18},{18,26},{... | collective-permute-start | bytes 147464 | tf_op jit(solution)/shard_map/ppermute | solution.py:16
  82.4 1.6 %collective-permute-start.14 = (f32[64,1,192]{2,0,1:T(8,128)}, f32[64,1,192]{2,0,1:T(8,128)S(1)}, u32[]{:S(2)}, u32[]{:S(2)}) collective-permute-start(f32[64,1,192]{2,0,1:T(8,128)} %get-tuple-element.16), channel_id=1, source_target_pairs={{0,2},{2,4},{4,6},{1,3},{3,5},{5,7},{8,10},{10,12},{12,14},{9,11},... | collective-permute-start | bytes 147464 | tf_op jit(solution)/shard_map/ppermute | solution.py:16
  84.0 1.3 collective-permute-start.15
  85.3 1.5 %collective-permute-start.16 = (f32[64,1,192]{2,0,1:T(8,128)S(1)}, f32[64,1,192]{2,0,1:T(8,128)S(1)}, u32[]{:S(2)}, u32[]{:S(2)}) collective-permute-start(f32[64,1,192]{2,0,1:T(8,128)S(1)} %get-tuple-element.14), channel_id=1, source_target_pairs={{0,1},{2,3},{4,5},{6,7},{8,9},{10,11},{12,13},{14,15},{16,17},{18,... | collective-permute-start | bytes 147464 | tf_op jit(solution)/shard_map/ppermute | solution.py:16
  86.8 1.3 collective-permute-start.17
  89.0 3.9 %collective-permute-done.17 = f32[64,1,192]{2,0,1:T(8,128)S(1)} collective-permute-done((f32[64,1,192]{2,0,1:T(8,128)S(1)}, f32[64,1,192]{2,0,1:T(8,128)S(1)}, u32[]{:S(2)}, u32[]{:S(2)}) %collective-permute-start.17) | collective-permute-done | bytes 49184 | tf_op jit(solution)/shard_map/ppermute | solution.py:17
  93.0 2.1 %convolution_bitcast_fusion = f32[64,6,192]{2,0,1:T(8,128)} fusion(bf16[1,1,1,6,192,192]{5,4,3,2,1,0:T(8,128)(2,1)} %param.7, f32[64,6,192]{2,0,1:T(8,128)S(1)} %copy.44, f32[64,6,192]{2,0,1:T(8,128)S(1)} %constant_dynamic-update-slice_fusion.12, f32[6]{0:T(128)S(1)} %stack.42), kind=kOutput, calls=%fused_computation.5 | convolution fusion | flops 28532736 | bytes 1327128 | tf_op jit(solution)/shard_map/rfa,fab->rfb/dot_general | solution.py:91
  97.3 4.4 %all-gather.3 = f32[2,64,8]{1,2,0:T(8,128)S(1)} all-gather(f32[1,64,8]{1,2,0:T(8,128)S(1)} %convolution_bitcast_fusion.3), channel_id=3, replica_groups=mesh['gx'=4,'gy'=4,'gz'=2] {'gz'}, dimensions={0}, use_global_device_ids=true | all-gather | bytes 6144 | tf_op jit(solution)/shard_map/all_gather | solution.py:60
  101.7 23.9 %all_gather.23 = f32[64,256]{0,1:T(8,128)S(1)} all-gather(f32[64,16]{0,1:T(8,128)S(1)} %bitcast.61), channel_id=1, replica_groups=mesh['gx'=4,'gy'=4,'gz'=2] {'gx','gy'}, dimensions={1}, use_global_device_ids=true | all-gather | bytes 69632 | tf_op jit(solution)/shard_map/all_gather | solution.py:61
  125.8 1.4 fusion.5
  127.2 1.3 collective-permute-start.18
  128.5 1.3 collective-permute-start.19
  129.8 2.2 %collective-permute-start.20 = (f32[64,1,192]{2,0,1:T(8,128)S(1)}, f32[64,1,192]{2,0,1:T(8,128)S(1)}, u32[]{:S(2)}, u32[]{:S(2)}) collective-permute-start(f32[64,1,192]{2,0,1:T(8,128)S(1)} %get-tuple-element.10), channel_id=1, source_target_pairs={{0,2},{2,4},{4,6},{1,3},{3,5},{5,7},{8,10},{10,12},{12,14},{9,11},... | collective-permute-start | bytes 147464 | tf_op jit(solution)/shard_map/ppermute | solution.py:16
  132.1 1.3 collective-permute-start.21
  133.4 1.9 %collective-permute-start.22 = (f32[64,1,192]{2,0,1:T(8,128)S(1)}, f32[64,1,192]{2,0,1:T(8,128)S(1)}, u32[]{:S(2)}, u32[]{:S(2)}) collective-permute-start(f32[64,1,192]{2,0,1:T(8,128)S(1)} %get-tuple-element.8), channel_id=1, source_target_pairs={{0,1},{2,3},{4,5},{6,7},{8,9},{10,11},{12,13},{14,15},{16,17},{18,... | collective-permute-start | bytes 147464 | tf_op jit(solution)/shard_map/ppermute | solution.py:16
  135.3 1.3 collective-permute-start.23
  137.6 4.4 %collective-permute-done.23 = f32[64,1,192]{2,0,1:T(8,128)S(1)} collective-permute-done((f32[64,1,192]{2,0,1:T(8,128)S(1)}, f32[64,1,192]{2,0,1:T(8,128)S(1)}, u32[]{:S(2)}, u32[]{:S(2)}) %collective-permute-start.23) | collective-permute-done | bytes 49184 | tf_op jit(solution)/shard_map/ppermute | solution.py:17
  (88 shorter events, 21.5 us)
Async XLA Ops:
  0.0 72.6 %copy-start = (bf16[1,1,1,1152,1152]{4,3,2,1,0:T(8,128)(2,1)S(1)}, bf16[1,1,1,1152,1152]{4,3,2,1,0:T(8,128)(2,1)}, u32[]{:S(2)}) copy-start(bf16[1,1,1,1152,1152]{4,3,2,1,0:T(8,128)(2,1)} %param.6) | copy-start | bytes 7962628
  1.4 22.9 %copy-start.4 = (bf16[1,1,1,8,1152]{4,3,2,1,0:T(8,128)(2,1)S(1)}, bf16[1,1,1,8,1152]{4,3,2,1,0:T(8,128)(2,1)}, u32[]{:S(2)}) copy-start(bf16[1,1,1,8,1152]{4,3,2,1,0:T(8,128)(2,1)} %param.8) | copy-start | bytes 55300
  1.4 52.6 %copy-start.5 = (bf16[1,1,1,8,256]{4,3,2,1,0:T(8,128)(2,1)S(1)}, bf16[1,1,1,8,256]{4,3,2,1,0:T(8,128)(2,1)}, u32[]{:S(2)}) copy-start(bf16[1,1,1,8,256]{4,3,2,1,0:T(8,128)(2,1)} %param.9) | copy-start | bytes 12292
  2.1 15.2 %collective-permute-start = (f32[64,1,192]{2,0,1:T(8,128)}, f32[64,1,192]{2,0,1:T(8,128)}, u32[]{:S(2)}, u32[]{:S(2)}) collective-permute-start(f32[64,1,192]{2,0,1:T(8,128)} %get-tuple-element.30), channel_id=1, source_target_pairs={{0,8},{8,16},{16,24},{1,9},{9,17},{17,25},{2,10},{10,18},{18,26},{... | collective-permute-start | bytes 147464 | tf_op jit(solution)/shard_map/ppermute | solution.py:16
  7.7 11.9 %collective-permute-start.1 = (f32[64,1,192]{2,0,1:T(8,128)}, f32[64,1,192]{2,0,1:T(8,128)}, u32[]{:S(2)}, u32[]{:S(2)}) collective-permute-start(f32[64,1,192]{2,0,1:T(8,128)} %get-tuple-element.29), channel_id=1, source_target_pairs={{8,0},{16,8},{24,16},{9,1},{17,9},{25,17},{10,2},{18,10},{26,18},{... | collective-permute-start | bytes 147464 | tf_op jit(solution)/shard_map/ppermute | solution.py:17
  9.0 11.4 %collective-permute-start.2 = (f32[64,1,192]{2,0,1:T(8,128)S(1)}, f32[64,1,192]{2,0,1:T(8,128)}, u32[]{:S(2)}, u32[]{:S(2)}) collective-permute-start(f32[64,1,192]{2,0,1:T(8,128)S(1)} %get-tuple-element.28), channel_id=1, source_target_pairs={{0,2},{2,4},{4,6},{1,3},{3,5},{5,7},{8,10},{10,12},{12,14},{9,11},... | collective-permute-start | bytes 147464 | tf_op jit(solution)/shard_map/ppermute | solution.py:16
  11.0 10.2 %collective-permute-start.3 = (f32[64,1,192]{2,0,1:T(8,128)S(1)}, f32[64,1,192]{2,0,1:T(8,128)}, u32[]{:S(2)}, u32[]{:S(2)}) collective-permute-start(f32[64,1,192]{2,0,1:T(8,128)S(1)} %get-tuple-element.27), channel_id=1, source_target_pairs={{2,0},{4,2},{6,4},{3,1},{5,3},{7,5},{10,8},{12,10},{14,12},{11,9},... | collective-permute-start | bytes 147464 | tf_op jit(solution)/shard_map/ppermute | solution.py:17
  12.3 9.8 %collective-permute-start.4 = (f32[64,1,192]{2,0,1:T(8,128)S(1)}, f32[64,1,192]{2,0,1:T(8,128)}, u32[]{:S(2)}, u32[]{:S(2)}) collective-permute-start(f32[64,1,192]{2,0,1:T(8,128)S(1)} %get-tuple-element.26), channel_id=1, source_target_pairs={{0,1},{2,3},{4,5},{6,7},{8,9},{10,11},{12,13},{14,15},{16,17},{18,... | collective-permute-start | bytes 147464 | tf_op jit(solution)/shard_map/ppermute | solution.py:16
  17.3 6.6 %copy-start.1 = (bf16[1,1,1,6,192,192]{5,4,3,2,1,0:T(8,128)(2,1)S(1)}, bf16[1,1,1,6,192,192]{5,4,3,2,1,0:T(8,128)(2,1)}, u32[]{:S(2)}) copy-start(bf16[1,1,1,6,192,192]{5,4,3,2,1,0:T(8,128)(2,1)} %param.7) | copy-start | bytes 1327108
  17.3 6.3 %collective-permute-start.5 = (f32[64,1,192]{2,0,1:T(8,128)S(1)}, f32[64,1,192]{2,0,1:T(8,128)S(1)}, u32[]{:S(2)}, u32[]{:S(2)}) collective-permute-start(f32[64,1,192]{2,0,1:T(8,128)S(1)} %get-tuple-element.25), channel_id=1, source_target_pairs={{1,0},{3,2},{5,4},{7,6},{9,8},{11,10},{13,12},{15,14},{17,16},{19,... | collective-permute-start | bytes 147464 | tf_op jit(solution)/shard_map/ppermute | solution.py:17
  24.3 48.3 %copy-start.3 = (bf16[1,1,1,64,1152]{4,3,2,1,0:T(8,128)(2,1)S(1)}, bf16[1,1,1,64,1152]{4,3,2,1,0:T(8,128)(2,1)}, u32[]{:S(2)}) copy-start(bf16[1,1,1,64,1152]{4,3,2,1,0:T(8,128)(2,1)} %param.5) | copy-start | bytes 442372
  54.6 10.1 %collective-permute-start.6 = (f32[64,1,192]{2,0,1:T(8,128)S(1)}, f32[64,1,192]{2,0,1:T(8,128)S(1)}, u32[]{:S(2)}, u32[]{:S(2)}) collective-permute-start(f32[64,1,192]{2,0,1:T(8,128)S(1)} %get-tuple-element.24), channel_id=1, source_target_pairs={{0,8},{8,16},{16,24},{1,9},{9,17},{17,25},{2,10},{10,18},{18,26},{... | collective-permute-start | bytes 147464 | tf_op jit(solution)/shard_map/ppermute | solution.py:16
  55.9 10.1 %collective-permute-start.7 = (f32[64,1,192]{2,0,1:T(8,128)S(1)}, f32[64,1,192]{2,0,1:T(8,128)S(1)}, u32[]{:S(2)}, u32[]{:S(2)}) collective-permute-start(f32[64,1,192]{2,0,1:T(8,128)S(1)} %get-tuple-element.23), channel_id=1, source_target_pairs={{8,0},{16,8},{24,16},{9,1},{17,9},{25,17},{10,2},{18,10},{26,18},{... | collective-permute-start | bytes 147464 | tf_op jit(solution)/shard_map/ppermute | solution.py:17
  57.2 8.9 %collective-permute-start.8 = (f32[64,1,192]{2,0,1:T(8,128)S(1)}, f32[64,1,192]{2,0,1:T(8,128)S(1)}, u32[]{:S(2)}, u32[]{:S(2)}) collective-permute-start(f32[64,1,192]{2,0,1:T(8,128)S(1)} %get-tuple-element.22), channel_id=1, source_target_pairs={{0,2},{2,4},{4,6},{1,3},{3,5},{5,7},{8,10},{10,12},{12,14},{9,11},... | collective-permute-start | bytes 147464 | tf_op jit(solution)/shard_map/ppermute | solution.py:16
  59.5 6.6 %collective-permute-start.9 = (f32[64,1,192]{2,0,1:T(8,128)S(1)}, f32[64,1,192]{2,0,1:T(8,128)S(1)}, u32[]{:S(2)}, u32[]{:S(2)}) collective-permute-start(f32[64,1,192]{2,0,1:T(8,128)S(1)} %get-tuple-element.21), channel_id=1, source_target_pairs={{2,0},{4,2},{6,4},{3,1},{5,3},{7,5},{10,8},{12,10},{14,12},{11,9},... | collective-permute-start | bytes 147464 | tf_op jit(solution)/shard_map/ppermute | solution.py:17
  60.8 6.3 %collective-permute-start.10 = (f32[64,1,192]{2,0,1:T(8,128)S(1)}, f32[64,1,192]{2,0,1:T(8,128)S(1)}, u32[]{:S(2)}, u32[]{:S(2)}) collective-permute-start(f32[64,1,192]{2,0,1:T(8,128)S(1)} %get-tuple-element.20), channel_id=1, source_target_pairs={{0,1},{2,3},{4,5},{6,7},{8,9},{10,11},{12,13},{14,15},{16,17},{18,... | collective-permute-start | bytes 147464 | tf_op jit(solution)/shard_map/ppermute | solution.py:16
  64.8 6.7 %collective-permute-start.11 = (f32[64,1,192]{2,0,1:T(8,128)S(1)}, f32[64,1,192]{2,0,1:T(8,128)S(1)}, u32[]{:S(2)}, u32[]{:S(2)}) collective-permute-start(f32[64,1,192]{2,0,1:T(8,128)S(1)} %get-tuple-element.19), channel_id=1, source_target_pairs={{1,0},{3,2},{5,4},{7,6},{9,8},{11,10},{13,12},{15,14},{17,16},{19,... | collective-permute-start | bytes 147464 | tf_op jit(solution)/shard_map/ppermute | solution.py:17
  76.1 10.7 %collective-permute-start.12 = (f32[64,1,192]{2,0,1:T(8,128)}, f32[64,1,192]{2,0,1:T(8,128)}, u32[]{:S(2)}, u32[]{:S(2)}) collective-permute-start(f32[64,1,192]{2,0,1:T(8,128)} %get-tuple-element.18), channel_id=1, source_target_pairs={{0,8},{8,16},{16,24},{1,9},{9,17},{17,25},{2,10},{10,18},{18,26},{... | collective-permute-start | bytes 147464 | tf_op jit(solution)/shard_map/ppermute | solution.py:16
  81.1 7.8 %collective-permute-start.13 = (f32[64,1,192]{2,0,1:T(8,128)}, f32[64,1,192]{2,0,1:T(8,128)S(1)}, u32[]{:S(2)}, u32[]{:S(2)}) collective-permute-start(f32[64,1,192]{2,0,1:T(8,128)} %get-tuple-element.17), channel_id=1, source_target_pairs={{8,0},{16,8},{24,16},{9,1},{17,9},{25,17},{10,2},{18,10},{26,18},{... | collective-permute-start | bytes 147464 | tf_op jit(solution)/shard_map/ppermute | solution.py:17
  82.4 6.6 %collective-permute-start.14 = (f32[64,1,192]{2,0,1:T(8,128)}, f32[64,1,192]{2,0,1:T(8,128)S(1)}, u32[]{:S(2)}, u32[]{:S(2)}) collective-permute-start(f32[64,1,192]{2,0,1:T(8,128)} %get-tuple-element.16), channel_id=1, source_target_pairs={{0,2},{2,4},{4,6},{1,3},{3,5},{5,7},{8,10},{10,12},{12,14},{9,11},... | collective-permute-start | bytes 147464 | tf_op jit(solution)/shard_map/ppermute | solution.py:16
  84.0 5.0 %collective-permute-start.15 = (f32[64,1,192]{2,0,1:T(8,128)}, f32[64,1,192]{2,0,1:T(8,128)S(1)}, u32[]{:S(2)}, u32[]{:S(2)}) collective-permute-start(f32[64,1,192]{2,0,1:T(8,128)} %get-tuple-element.15), channel_id=1, source_target_pairs={{2,0},{4,2},{6,4},{3,1},{5,3},{7,5},{10,8},{12,10},{14,12},{11,9},... | collective-permute-start | bytes 147464 | tf_op jit(solution)/shard_map/ppermute | solution.py:17
  85.3 3.7 %collective-permute-start.16 = (f32[64,1,192]{2,0,1:T(8,128)S(1)}, f32[64,1,192]{2,0,1:T(8,128)S(1)}, u32[]{:S(2)}, u32[]{:S(2)}) collective-permute-start(f32[64,1,192]{2,0,1:T(8,128)S(1)} %get-tuple-element.14), channel_id=1, source_target_pairs={{0,1},{2,3},{4,5},{6,7},{8,9},{10,11},{12,13},{14,15},{16,17},{18,... | collective-permute-start | bytes 147464 | tf_op jit(solution)/shard_map/ppermute | solution.py:16
  86.8 6.2 %collective-permute-start.17 = (f32[64,1,192]{2,0,1:T(8,128)S(1)}, f32[64,1,192]{2,0,1:T(8,128)S(1)}, u32[]{:S(2)}, u32[]{:S(2)}) collective-permute-start(f32[64,1,192]{2,0,1:T(8,128)S(1)} %get-tuple-element.13), channel_id=1, source_target_pairs={{1,0},{3,2},{5,4},{7,6},{9,8},{11,10},{13,12},{15,14},{17,16},{19,... | collective-permute-start | bytes 147464 | tf_op jit(solution)/shard_map/ppermute | solution.py:17
  96.2 45.9 %copy-start.2 = (f32[64,6,192]{2,0,1:T(8,128)S(1)}, f32[64,6,192]{2,0,1:T(8,128)}, u32[]{:S(2)}) copy-start(f32[64,6,192]{2,0,1:T(8,128)} %get-tuple-element.6) | copy-start | bytes 884740
  127.2 8.1 %collective-permute-start.18 = (f32[64,1,192]{2,0,1:T(8,128)S(1)}, f32[64,1,192]{2,0,1:T(8,128)S(1)}, u32[]{:S(2)}, u32[]{:S(2)}) collective-permute-start(f32[64,1,192]{2,0,1:T(8,128)S(1)} %get-tuple-element.12), channel_id=1, source_target_pairs={{0,8},{8,16},{16,24},{1,9},{9,17},{17,25},{2,10},{10,18},{18,26},{... | collective-permute-start | bytes 147464 | tf_op jit(solution)/shard_map/ppermute | solution.py:16
  128.5 8.1 %collective-permute-start.19 = (f32[64,1,192]{2,0,1:T(8,128)S(1)}, f32[64,1,192]{2,0,1:T(8,128)S(1)}, u32[]{:S(2)}, u32[]{:S(2)}) collective-permute-start(f32[64,1,192]{2,0,1:T(8,128)S(1)} %get-tuple-element.11), channel_id=1, source_target_pairs={{8,0},{16,8},{24,16},{9,1},{17,9},{25,17},{10,2},{18,10},{26,18},{... | collective-permute-start | bytes 147464 | tf_op jit(solution)/shard_map/ppermute | solution.py:17
  129.8 6.8 %collective-permute-start.20 = (f32[64,1,192]{2,0,1:T(8,128)S(1)}, f32[64,1,192]{2,0,1:T(8,128)S(1)}, u32[]{:S(2)}, u32[]{:S(2)}) collective-permute-start(f32[64,1,192]{2,0,1:T(8,128)S(1)} %get-tuple-element.10), channel_id=1, source_target_pairs={{0,2},{2,4},{4,6},{1,3},{3,5},{5,7},{8,10},{10,12},{12,14},{9,11},... | collective-permute-start | bytes 147464 | tf_op jit(solution)/shard_map/ppermute | solution.py:16
  132.1 4.6 %collective-permute-start.21 = (f32[64,1,192]{2,0,1:T(8,128)S(1)}, f32[64,1,192]{2,0,1:T(8,128)S(1)}, u32[]{:S(2)}, u32[]{:S(2)}) collective-permute-start(f32[64,1,192]{2,0,1:T(8,128)S(1)} %get-tuple-element.9), channel_id=1, source_target_pairs={{2,0},{4,2},{6,4},{3,1},{5,3},{7,5},{10,8},{12,10},{14,12},{11,9},... | collective-permute-start | bytes 147464 | tf_op jit(solution)/shard_map/ppermute | solution.py:17
  133.4 4.2 %collective-permute-start.22 = (f32[64,1,192]{2,0,1:T(8,128)S(1)}, f32[64,1,192]{2,0,1:T(8,128)S(1)}, u32[]{:S(2)}, u32[]{:S(2)}) collective-permute-start(f32[64,1,192]{2,0,1:T(8,128)S(1)} %get-tuple-element.8), channel_id=1, source_target_pairs={{0,1},{2,3},{4,5},{6,7},{8,9},{10,11},{12,13},{14,15},{16,17},{18,... | collective-permute-start | bytes 147464 | tf_op jit(solution)/shard_map/ppermute | solution.py:16
  135.3 6.7 %collective-permute-start.23 = (f32[64,1,192]{2,0,1:T(8,128)S(1)}, f32[64,1,192]{2,0,1:T(8,128)S(1)}, u32[]{:S(2)}, u32[]{:S(2)}) collective-permute-start(f32[64,1,192]{2,0,1:T(8,128)S(1)} %get-tuple-element.7), channel_id=1, source_target_pairs={{1,0},{3,2},{5,4},{7,6},{9,8},{11,10},{13,12},{15,14},{17,16},{19,... | collective-permute-start | bytes 147464 | tf_op jit(solution)/shard_map/ppermute | solution.py:17
